TPU v7x, 32 devices: a whole 2x2x4 slice. The times are simulated.
32 devices in a mesh: groups: 2 (over y), gz: 4 (over z), xy: 2 (over x), col: 2 (over core).
Axes of the slice: x: 2, y: 2, z: 4, core: 2. Of those that a mesh axis runs over, the one named last changes fastest.
Arguments:
- features: bfloat16 [8, 16, 256, 256], P(('groups', 'gz'), None, ('xy', 'col')), parts along dimension 0, may hold values from -24 to 24
- class_map: int32 [8, 256, 256], P(('groups', 'gz'), ('xy', 'col')), parts along dimension 0, may hold values from 0 to 3
- stiffness: float32 [4], replicated, may hold values from 0.2 to 2
- valid: int32 [8, 4], P('groups'), parts along dimension 0, may hold values 0 or 1
Outputs:
- displacement: float32 [8, 2, 256, 256], P(('groups', 'gz'), None, ('xy', 'col')), parts along dimension 0
- forward_flow: float32 [8, 2, 256, 256], P(('groups', 'gz'), None, ('xy', 'col')), parts along dimension 0
There are 2 independent parts, one for each index of `groups`. A program takes and returns all parts, laid end to end along the dimension named above; an argument that names none is the same for every part. Nothing has to cross between parts.
All inputs are finite; a program needn't handle non-finite values.
Results may differ from a plain program's by a relative error of at most 0.0017.
Values may be sent and summed in bfloat16 or wider, within the bound.
No kernel may reach another device: no remote copies, remote signals or barrier semaphores. Data moves between devices by JAX's collectives and lax.ppermute only.
A program may use at most 64 MiB of HBM per device.

v0:
```python
import functools

import jax
import jax.numpy as jnp
from jax import lax
from jax.experimental import pallas as pl
from jax.experimental.pallas import tpu as pltpu
from jax.sharding import PartitionSpec as P

RADIUS = 6
STEPS = 3
score_scale = 0.25
step_size = 0.1
saturation = 2.0
tile_axes = ("xy", "col")


def ringed(value, axis, steps):
    count = lax.axis_size(axis)
    return lax.ppermute(value, axis, [(i, (i + steps) % count) for i in range(count)])


BLOCK = 4
SPAN = BLOCK + 2 * RADIUS
GROUP = 32
LOG2E = 1.4426950408889634
MASKED = -1e30


def flow_kernel(
    early_rows, late_rows, n_early, live_ref, *refs
):
    n_in = n_early + 1 + max(i for i, _ in late_rows)
    ins, out_ref = refs[:n_in], refs[n_in]
    t_ref, bias_ref, o_ref, s0_ref, s1_ref, s2_ref, s3_ref, w_ref = refs[n_in + 1 :]
    channels, breadth = ins[0].shape[1:]
    groups = 1
    steps = breadth // BLOCK // 2
    wide = t_ref.shape[3]
    lane = lax.broadcasted_iota(jnp.int32, (8, 128), 1)
    sub = lax.broadcasted_iota(jnp.int32, (8, 128), 0)
    qc = lane // GROUP
    qr = lane % GROUP // (GROUP // BLOCK)
    col_ok = []
    for half in range(2):
        kc = sub + 8 * half
        col_ok.append((kc >= qc) & (kc <= qc + 2 * RADIUS))
    edge = [k for k in range(SPAN) if k < BLOCK - 1 or k > 2 * RADIUS]
    for n, kr in enumerate(edge):
        row_ok = (qr <= kr) & (kr <= qr + 2 * RADIUS)
        for half in range(2):
            bias_ref[2 * n + half] = jnp.where(row_ok & col_ok[half], 0.0, MASKED)
    place = jnp.where(
        lax.broadcasted_iota(jnp.int32, (wide, breadth), 0)
        == lax.broadcasted_iota(jnp.int32, (wide, breadth), 1) + RADIUS,
        1.0,
        0.0,
    ).astype(jnp.bfloat16)
    per = GROUP // BLOCK
    for side, (offset, table) in enumerate(((0, early_rows), (n_early, late_rows))):
        for g in range(groups):
            for kr in range(0, SPAN, 2):
                pieces = []
                for k in range(2):
                    for b in range(per):
                        which, row = table[SPAN * b + kr + k]
                        pieces.append(ins[offset + which][row])
                flat = jnp.concatenate(pieces, axis=0)
                out = lax.dot_general(
                    place, flat, (((1,), (1,)), ((), ())), preferred_element_type=jnp.float32
                )
                t_ref[side, g, kr] = out[:, :128]
                t_ref[side, g, kr + 1] = out[:, 128:]

    diagonal = lane // channels == sub
    zero_b = jnp.zeros((16, 128), jnp.bfloat16)
    for side in range(2):

        def tiles_of(i):
            tiles = []
            for k in range(2):
                g = 0
                base = i * BLOCK + k * (breadth // 2)
                tiles.append((g, base))
            return tiles

        def score(i, s_ref):
            tiles = tiles_of(i)
            keys = []
            for kr in range(SPAN):
                keys.append(
                    jnp.concatenate(
                        [t_ref[1 - side, g, kr, pl.ds(base, SPAN), :] for g, base in tiles], axis=1
                    ).astype(jnp.bfloat16)
                )
            keys = jnp.concatenate(keys, axis=0)
            parts = []
            for k, (g, base) in enumerate(tiles):
                for c in range(BLOCK):
                    for r in range(0, BLOCK, 2):
                        pair = [
                            jnp.where(
                                diagonal,
                                t_ref[side, g, RADIUS + r + m, pl.ds(base + RADIUS + c, 1), :],
                                0.0,
                            )
                            for m in range(2)
                        ]
                        sel = jnp.concatenate(pair, axis=0).astype(jnp.bfloat16)
                        parts.append(
                            jnp.concatenate([sel, zero_b] if k == 0 else [zero_b, sel], axis=1)
                        )
            queries = jnp.concatenate(parts, axis=0)
            s_ref[...] = lax.dot_general(
                keys, queries, (((1,), (1,)), ((), ())), preferred_element_type=jnp.float32
            )

        def settle(i, s_ref):
            for k, (g, base) in enumerate(tiles_of(i)):
                s = {}
                for kr in range(SPAN):
                    for half in range(2):
                        s[kr, half] = s_ref[
                            SPAN * kr + 8 * half : SPAN * kr + 8 * half + 8, 128 * k : 128 * k + 128
                        ]
                for n, kr in enumerate(edge):
                    for half in range(2):
                        s[kr, half] = s[kr, half] + bias_ref[2 * n + half]
                peak = []
                for half in range(2):
                    inner = functools.reduce(
                        jnp.maximum, [s[kr, half] for kr in range(SPAN) if kr not in edge]
                    )
                    inner = jnp.where(col_ok[half], inner, MASKED)
                    peak.append(
                        functools.reduce(jnp.maximum, [s[kr, half] for kr in edge] + [inner])
                    )
                top = jnp.max(jnp.maximum(peak[0], peak[1]), axis=0, keepdims=True)
                top = jnp.broadcast_to(top, (8, 128))
                total, slope = [], []
                for half in range(2):
                    acc = None
                    mom = None
                    for kr in reversed(range(SPAN)):
                        w = jnp.exp2((s[kr, half] - top) * (LOG2E * score_scale))
                        acc = w if acc is None else acc + w
                        if kr > 0:
                            mom = acc if mom is None else mom + acc
                    total.append(jnp.where(col_ok[half], acc, 0.0))
                    slope.append(jnp.where(col_ok[half], mom, 0.0))
                both = total[0] + total[1]
                den = jnp.sum(both, axis=0, keepdims=True)
                row_sum = jnp.sum(slope[0] + slope[1], axis=0, keepdims=True)
                col_sum = jnp.sum(
                    both * sub.astype(jnp.float32) + 8.0 * total[1], axis=0, keepdims=True
                )
                fr = row_sum / den - (qr[0:1] + RADIUS).astype(jnp.float32)
                fc = col_sum / den - (qc[0:1] + RADIUS).astype(jnp.float32)
                both_f = jnp.concatenate([fr, fc], axis=0)
                for c in range(BLOCK):
                    r = both_f if c == 0 else pltpu.roll(both_f, 128 - GROUP * c, 1)
                    o_ref[side, 0, g, pl.ds(base + c, 1), :] = r[0:1]
                    o_ref[side, 1, g, pl.ds(base + c, 1), :] = r[1:2]

        def step(j, carry):
            last = steps - 1
            score(4 * j + 2, s2_ref)
            settle(4 * j, s0_ref)
            score(4 * j + 3, s3_ref)
            settle(4 * j + 1, s1_ref)
            score(jnp.minimum(4 * j + 4, last), s0_ref)
            settle(4 * j + 2, s2_ref)
            score(jnp.minimum(4 * j + 5, last), s1_ref)
            settle(4 * j + 3, s3_ref)
            return carry

        score(0, s0_ref)
        score(1, s1_ref)
        lax.fori_loop(0, steps // 4, step, 0)
    live = live_ref[0]
    for side in range(2):
        for comp in range(2):
            turned = jnp.transpose(o_ref[side, comp, 0], (1, 0)) * live
            for t in range(breadth // 128):
                for r in range(BLOCK):
                    w_ref[side, comp, t, pl.ds(r, per, stride=BLOCK), :] = turned[
                        per * r : per * r + per, 128 * t : 128 * t + 128
                    ]
                out_ref[2 * side + comp, :, 128 * t : 128 * t + 128] = w_ref[side, comp, t]


def flows(live, early, late, early_at, late_at, starts):
    _, breadth = early[0].shape[1:]
    wide = breadth + 16
    tables = [
        [at(start - RADIUS + k) for start in starts for k in range(SPAN)]
        for at in (early_at, late_at)
    ]
    cells = GROUP * breadth
    return pl.pallas_call(
        functools.partial(flow_kernel, *tables, len(early)),
        out_shape=jax.ShapeDtypeStruct((4, GROUP, breadth), jnp.float32),
        in_specs=[pl.BlockSpec(memory_space=pltpu.SMEM)]
        + [pl.BlockSpec(memory_space=pltpu.VMEM)] * (len(early) + len(late)),
        out_specs=pl.BlockSpec(memory_space=pltpu.VMEM),
        scratch_shapes=[
            pltpu.VMEM((2, 1, SPAN, wide, 128), jnp.float32),
            pltpu.VMEM((12, 8, 128), jnp.float32),
            pltpu.VMEM((2, 2, 1, breadth, 128), jnp.float32),
        ]
        + [pltpu.VMEM((SPAN * SPAN, 256), jnp.float32)] * 4
        + [pltpu.VMEM((2, 2, breadth // 128, GROUP, 128), jnp.float32)],
        compiler_params=pltpu.CompilerParams(vmem_limit_bytes=24 * 2**20),
        cost_estimate=pl.CostEstimate(
            flops=2 * cells * SPAN * SPAN * 2 * 256, bytes_accessed=2**22, transcendentals=2 * cells * SPAN * SPAN
        ),
        name="flows",
    )(live, *early, *late)


def spring(vector):
    squares = jnp.sum(vector * vector, axis=0, keepdims=True)
    return vector / jnp.sqrt(1.0 + squares / (saturation * saturation))


def pair_part(apart, here, forward, ahead):
    return step_size * here * (spring(apart - forward) - spring(-apart - ahead))


def split(value):
    high = lax.reduce_precision(value, 8, 7)
    return [high.astype(jnp.bfloat16), (value - high).astype(jnp.bfloat16)]


def running(gain, section):
    count = lax.axis_size("gz")
    reach = 1
    while count > 4 and reach < count - 2:
        more = jnp.where(section >= reach, ringed(gain, "gz", reach), 0.0)
        gain, reach = gain + more, 2 * reach
    return gain


def messages(flow, here, section):
    forward, ahead = flow[:2], flow[2:]
    gain = here * (forward - ahead)
    part = pair_part(0.5 * gain, here, forward, ahead).astype(jnp.bfloat16)
    halves = split(gain)
    to_next = jnp.concatenate([*halves, forward.astype(jnp.bfloat16)])
    to_second = jnp.concatenate([*split(running(gain, section)), part])
    return to_next, to_second, jnp.concatenate([part, *halves])


FRAME = 8


def spring_pair(row, col):
    length = jnp.sqrt(1.0 + (row * row + col * col) / (saturation * saturation))
    return row / length, col / length


def pair_pull(apart, here, forward, ahead):
    one = spring_pair(*[a - f for a, f in zip(apart, forward)])
    two = spring_pair(*[-a - b for a, b in zip(apart, ahead)])
    return [step_size * here * (x - y) for x, y in zip(one, two)]


def beside(value, edges):
    first, last = edges
    rows, cols = value.shape
    return (
        pltpu.roll(value, rows - 1, 0),
        pltpu.roll(value, 1, 0),
        jnp.where(last, 0.0, pltpu.roll(value, cols - 1, 1)),
        jnp.where(first, 0.0, pltpu.roll(value, 1, 1)),
    )


def springs_of(stiff, edges):
    return [0.5 * (stiff + s) for s in beside(stiff, edges)]


def eased(u, weights, inside, edges):
    out = []
    for part in u:
        total = 0.0
        for w, n in zip(weights, beside(part, edges)):
            total = total + w * (part - n)
        out.append(jnp.where(inside, part - step_size * total, 0.0))
    return out


def early_kernel(
    links_ref, stiffness_ref, depth_ref, middle_ref, edge_ref, below_mid_ref, below_out_ref, before_mid_ref,
    before_out_ref, above_mid_ref, above_out_ref, own_ref, upper_ref, lower_ref, change_ref, state_ref, frame_ref
):
    rows, cols = state_ref.shape[1:]
    height, thick = rows - 2 * FRAME, middle_ref.shape[1]
    side = edge_ref.shape[1] // 2
    top, low = FRAME - STEPS, FRAME + (height - thick) // 2

    def framed(mid, out):
        frame_ref[top : top + side] = out[:side]
        frame_ref[low : low + thick] = mid
        frame_ref[low + thick : low + thick + side] = out[side:]
        return frame_ref[...]

    def fields(mid_ref, out_ref, at):
        return [
            framed(mid_ref[i].astype(jnp.float32), out_ref[i].astype(jnp.float32))
            for i in range(at, at + 2)
        ]

    def coded(ref):
        frame_ref[...] = jnp.zeros((rows, cols), jnp.float32)
        frame_ref[top : top + height + 2 * STEPS] = ref[...].astype(jnp.float32)[: height + 2 * STEPS]
        code = frame_ref[...]
        stiff = jnp.zeros((rows, cols), jnp.float32)
        for k in range(stiffness_ref.shape[0]):
            stiff = jnp.where(code == k + 1.0, stiffness_ref[k], stiff)
        return stiff, code > 0.0

    row = lax.broadcasted_iota(jnp.int32, (rows, cols), 0)
    col = lax.broadcasted_iota(jnp.int32, (rows, cols), 1)
    edges = (col == 0, col == cols - 1)

    def linked(k):
        outer = jnp.where(row < FRAME, links_ref[k, 0], links_ref[k, 2])
        return jnp.where((row >= FRAME) & (row < FRAME + height), links_ref[k, 1], outer)

    below, here = linked(0), linked(1)
    stiff, inside = coded(own_ref)
    stiff_up, inside_up = coded(upper_ref)
    stiff_down, inside_down = coded(lower_ref)
    fwd, ahd = fields(middle_ref, edge_ref, 0), fields(middle_ref, edge_ref, 2)
    gain = [here * (f - a) for f, a in zip(fwd, ahd)]
    high, rest = fields(below_mid_ref, below_out_ref, 0), fields(below_mid_ref, below_out_ref, 2)
    gain_below = [h + r for h, r in zip(high, rest)]
    pri = fields(below_mid_ref, below_out_ref, 4)
    bwd = [p - g for p, g in zip(pri, gain_below)]
    high, rest = fields(before_mid_ref, before_out_ref, 0), fields(before_mid_ref, before_out_ref, 2)
    far = [jnp.where(depth_ref[0] > 1, h + r, 0.0) for h, r in zip(high, rest)]
    part_before = fields(before_mid_ref, before_out_ref, 4)
    part_above = fields(above_mid_ref, above_out_ref, 0)
    if above_mid_ref.shape[0] > 2:
        high, rest = fields(above_mid_ref, above_out_ref, 2), fields(above_mid_ref, above_out_ref, 4)
        far = [f + jnp.where(depth_ref[0] > 2, h + r, 0.0) for f, h, r in zip(far, high, rest)]

    start = [0.5 * (f + g) for f, g in zip(far, gain_below)]
    start_up = [s + 0.5 * g for s, g in zip(start, gain)]
    start_down = [s - 0.5 * g for s, g in zip(start, gain_below)]
    part = pair_pull([0.5 * g for g in gain], here, fwd, ahd)
    part_below = pair_pull([0.5 * g for g in gain_below], below, pri, bwd)

    weights = springs_of(stiff, edges)
    first = eased(start, weights, inside, edges)
    first = [u + p - q for u, p, q in zip(first, part, part_below)]
    first_up = eased(start_up, springs_of(stiff_up, edges), inside_up, edges)
    first_up = [u + p - q for u, p, q in zip(first_up, part_above, part)]
    first_down = eased(start_down, springs_of(stiff_down, edges), inside_down, edges)
    first_down = [u + p - q for u, p, q in zip(first_down, part_below, part_before)]
    pull = pair_pull([a - b for a, b in zip(first_up, first)], here, fwd, ahd)
    push = pair_pull([a - b for a, b in zip(first, first_down)], below, pri, bwd)
    second = [
        u + p - q for u, p, q in zip(eased(first, weights, inside, edges), pull, push)
    ]
    for i in range(2):
        change_ref[i] = (second[i] - start[i])[FRAME : FRAME + height].astype(jnp.bfloat16)
    for i, value in enumerate([*second, *start_up, *start_down, *fwd, *ahd, *pri, *bwd, here, below, stiff]):
        state_ref[i] = value


def late_kernel(up_ref, down_ref, state_ref, out_ref):
    rows, cols = state_ref.shape[1:]
    height = rows - 2 * FRAME
    body = slice(FRAME, FRAME + height)
    col = lax.broadcasted_iota(jnp.int32, (rows, cols), 1)
    edges = (col == 0, col == cols - 1)
    second = [state_ref[i] for i in range(2)]
    stiff = state_ref[16]
    third = eased(second, springs_of(stiff, edges), stiff > 0.0, edges)

    def two(at):
        return [state_ref[at + i, body, :] for i in range(2)]

    mid = two(0)
    up = [a + up_ref[i].astype(jnp.float32) - m for i, (a, m) in enumerate(zip(two(2), mid))]
    down = [m - a - down_ref[i].astype(jnp.float32) for i, (a, m) in enumerate(zip(two(4), mid))]
    pull = pair_pull(up, state_ref[14, body, :], two(6), two(8))
    push = pair_pull(down, state_ref[15, body, :], two(10), two(12))
    for i in range(2):
        out_ref[i] = third[i][body] + pull[i] - push[i]


def relaxation(change_shape, links, stiffness, depth, arrays):
    height, breadth = change_shape[1:]
    vmem, smem = pl.BlockSpec(memory_space=pltpu.VMEM), pl.BlockSpec(memory_space=pltpu.SMEM)
    change, state = pl.pallas_call(
        early_kernel,
        out_shape=(
            jax.ShapeDtypeStruct(change_shape, jnp.bfloat16),
            jax.ShapeDtypeStruct((17, height + 2 * FRAME, breadth), jnp.float32),
        ),
        in_specs=[smem] * 3 + [vmem] * len(arrays),
        out_specs=(vmem, vmem),
        scratch_shapes=[pltpu.VMEM((height + 2 * FRAME, breadth), jnp.float32)],
        compiler_params=pltpu.CompilerParams(vmem_limit_bytes=16 * 2**20),
        cost_estimate=pl.CostEstimate(flops=2**23, bytes_accessed=2**21, transcendentals=2**16),
        name="early_steps",
    )(links, stiffness, depth, *arrays)
    up, down = ringed(change, "gz", -1), ringed(change, "gz", 1)
    return pl.pallas_call(
        late_kernel,
        out_shape=jax.ShapeDtypeStruct(change_shape, jnp.float32),
        in_specs=[vmem] * 3,
        out_specs=vmem,
        compiler_params=pltpu.CompilerParams(vmem_limit_bytes=16 * 2**20),
        cost_estimate=pl.CostEstimate(flops=2**22, bytes_accessed=2**21, transcendentals=2**15),
        name="last_step",
    )(up, down, state)


def whole_device(features, class_map, stiffness, valid):
    center = jnp.transpose(features[0], (1, 0, 2))
    height, channels, breadth = center.shape
    section, sections = lax.axis_index("gz"), lax.axis_size("gz")
    tile, tiles = lax.axis_index(tile_axes), lax.axis_size(tile_axes)
    quarter = height // 4
    low, high = quarter - RADIUS, height - quarter + RADIUS

    upper_mid = ringed(center[low:high], "gz", -1)

    codes = (class_map[0] + 1).astype(jnp.bfloat16).reshape(-1, channels, breadth)
    top = jnp.concatenate([center[:RADIUS], codes[:1]])
    bottom = jnp.concatenate([center[-RADIUS:], codes[-1:]])
    nothing = jnp.zeros_like(top)
    before = jnp.where(tile > 0, ringed(bottom, tile_axes, 1), nothing)
    after = jnp.where(tile < tiles - 1, ringed(top, tile_axes, -1), nothing)
    own_codes = jnp.concatenate(
        [before[RADIUS, -STEPS:], codes.reshape(height, breadth), after[RADIUS, :STEPS]]
    )
    spare = -own_codes.shape[0] % channels
    packed = jnp.pad(own_codes, ((0, spare), (0, 0))).reshape(-1, channels, breadth)
    upper_out = ringed(
        jnp.concatenate([before[:RADIUS], center[:low], center[high:], after[:RADIUS], packed]),
        "gz",
        -1,
    )
    outer = low + RADIUS
    upper_codes = upper_out[2 * outer :].reshape(-1, breadth)[: own_codes.shape[0]]

    def own_at(row):
        if row < 0:
            return 1, row + RADIUS
        return (0, row) if row < height else (2, row - height)

    def upper_at(row):
        if low <= row < high:
            return 0, row - low
        return (1, row + RADIUS) if row < low else (1, row - high + outer)

    sound = jnp.pad(valid.astype(jnp.float32), ((1, 1), (1, 1)))
    near = lax.dynamic_slice(sound, (section, tile), (3, 3))
    links = near[:-1] * near[1:]
    by_row = jnp.concatenate(
        [
            jnp.broadcast_to(links[:, k : k + 1], (2, count))
            for k, count in enumerate((STEPS, height, STEPS))
        ],
        axis=1,
    )

    def own_links(begin, count):
        return by_row[1][None, begin : begin + count, None]

    live = jnp.where(section < sections - 1, 1.0, 0.0)[None]
    middle_rows = range(quarter, height - quarter, BLOCK)
    middle = flows(live, [center], [upper_mid], own_at, upper_at, middle_rows)
    by_mid = own_links(quarter + STEPS, height // 2)
    sent_mid = messages(middle, by_mid, section)
    n_mid = 6 * middle.shape[1]
    below_mid = ringed(jnp.concatenate([sent_mid[0].reshape(n_mid, breadth), own_codes]), "gz", 1)
    before_mid = ringed(sent_mid[1], "gz", 2)
    above_mid = ringed(sent_mid[2], "gz", -1)
    outer_rows = [*range(0, quarter, BLOCK), *range(height - quarter, height, BLOCK)]
    outside = flows(
        live, [center, before, after], [upper_mid, upper_out], own_at, upper_at, outer_rows
    )

    head, tail = outside[:, :quarter], outside[:, quarter:]
    head = jnp.concatenate([ringed(tail[:, -STEPS:], tile_axes, 1), head], axis=1)
    tail = jnp.concatenate([tail, ringed(outside[:, :STEPS], tile_axes, -1)], axis=1)
    edge_rows = jnp.concatenate([head, tail], axis=1)
    first_tail = head.shape[1]
    by_edge = jnp.concatenate(
        [own_links(0, first_tail), own_links(height + 2 * STEPS - first_tail, first_tail)], axis=1
    )
    sent_out = messages(edge_rows, by_edge, section)
    below_out = ringed(sent_out[0], "gz", 1)
    before_out = ringed(sent_out[1], "gz", 2)
    above_out = ringed(sent_out[2], "gz", -1)

    forward = jnp.concatenate(
        [outside[:2, :quarter], middle[:2], outside[:2, quarter:]], axis=1
    )
    arrays = [
        middle,
        edge_rows,
        below_mid[:n_mid].reshape(6, -1, breadth),
        below_out,
        before_mid,
        before_out,
        above_mid,
        above_out,
        own_codes,
        upper_codes,
        below_mid[n_mid:],
    ]
    third = relaxation((2, height, breadth), links, stiffness, section[None], arrays)
    return (third[None], forward[None])


def solution(mesh):
    placed = (
        P(("groups", "gz"), None, tile_axes, None),
        P(("groups", "gz"), tile_axes, None),
        P(),
        P("groups", None),
    )
    return jax.shard_map(
        whole_device,
        mesh=mesh,
        in_specs=placed,
        out_specs=(P(("groups", "gz"), None, tile_axes, None),) * 2,
        check_vma=False,
    )
```

profile of v0, /device:TPU:0, one launch (start us, length us, event | category | flops | bytes accessed | tf_op | source)
XLA Modules:
  0.0 78.0 jit_solution(3244897195638130634)
XLA Ops:
  0.6 0.9 %add_convert_fusion = bf16[1,64,256]{2,1,0:T(8,128)(2,1)S(1)} fusion(s32[1,64,256]{2,1,0:T(8,128)} %param.5), kind=kLoop, calls=%fused_computation.32 | loop fusion | flops 32768 | bytes 98304 | tf_op jit(solution)/shard_map/convert_element_type | solution.py:433
  1.6 1.3 %copy.9 = bf16[1,16,64,256]{3,1,2,0:T(8,128)(2,1)S(1)} copy(bf16[1,16,64,256]{3,2,1,0:T(8,128)(2,1)} %param.4) | data formatting | bytes 1048576 | tf_op args[0]
  2.9 0.5 collective-permute-start.1
  3.5 2.0 %collective-permute-start.2 = (bf16[7,16,256]{2,1,0:T(8,128)(2,1)S(1)}, bf16[7,16,256]{2,1,0:T(8,128)(2,1)S(1)}, u32[]{:S(2)}, u32[]{:S(2)}) collective-permute-start(bf16[7,16,256]{2,1,0:T(8,128)(2,1)S(1)} %pad_maximum_fusion.11), channel_id=1, source_target_pairs={{0,3},{1,0},{2,1},{3,2},{4,7},{5,4},{6,5},{7,6},{8,11},{9,8},{10,9... | collective-permute-start | bytes 172040 | tf_op jit(solution)/shard_map/ppermute | solution.py:20
  5.5 4.4 %collective-permute-start = (bf16[44,16,256]{2,1,0:T(8,128)(2,1)S(1)}, bf16[44,16,256]{2,1,0:T(8,128)(2,1)S(1)}, u32[]{:S(2)}, u32[]{:S(2)}) collective-permute-start(bf16[44,16,256]{2,1,0:T(8,128)(2,1)S(1)} %slice.151), channel_id=1, source_target_pairs={{0,12},{4,0},{8,4},{12,8},{1,13},{5,1},{9,5},{13,9},{2,14},{6,2},{... | collective-permute-start | bytes 1081352 | tf_op jit(solution)/shard_map/ppermute | solution.py:20
  10.0 0.6 slice.134
  12.7 6.0 %collective-permute-done.refs_1_.refs_3_ = bf16[44,16,256]{2,1,0:T(8,128)(2,1)S(1)} collective-permute-done((bf16[44,16,256]{2,1,0:T(8,128)(2,1)S(1)}, bf16[44,16,256]{2,1,0:T(8,128)(2,1)S(1)}, u32[]{:S(2)}, u32[]{:S(2)}) %collective-permute-start) | collective-permute-done | bytes 360480 | tf_op jit(solution)/shard_map/ppermute | solution.py:20
  18.7 11.3 %flows.2.middle_ref = f32[4,32,256]{2,1,0:T(8,128)S(1)} custom-call(f32[1]{0:T(128)} %bitcast.1.live_ref, bf16[64,16,256]{2,1,0:T(8,128)(2,1)S(1)} %bitcast.36, bf16[44,16,256]{2,1,0:T(8,128)(2,1)S(1)} %collective-permute-done.refs_1_.refs_3_), custom_call_target="tpu_custom_call" | custom-call | flops 2147483648 | bytes 4194304 | tf_op jit(solution)/shard_map/flows/pallas_call | solution.py:200
  30.0 0.6 multiply_reduce_fusion.3
  30.8 11.3 %flows.3 = f32[4,32,256]{2,1,0:T(8,128)S(1)} custom-call(f32[1]{0:T(128)} %bitcast.1.live_ref, bf16[64,16,256]{2,1,0:T(8,128)(2,1)S(1)} %bitcast.37, bf16[7,16,256]{2,1,0:T(8,128)(2,1)S(1)} %broadcast_select_fusion.1.refs_1_, bf16[7,16,256]{2,1,0:T(8,128)(2,1)S(1)} %broadcast_select_fusion.refs_2_, ...), custom_call_target="tpu_custom_call" | custom-call | flops 2147483648 | bytes 4194304 | tf_op jit(solution)/shard_map/flows/pallas_call | solution.py:200
  42.2 1.7 %collective-permute-start.5 = (f32[4,3,256]{2,1,0:T(4,128)S(1)}, f32[4,3,256]{2,1,0:T(4,128)S(1)}, u32[]{:S(2)}, u32[]{:S(2)}) collective-permute-start(f32[4,3,256]{2,1,0:T(4,128)S(1)} %get-tuple-element.22), channel_id=1, source_target_pairs={{0,3},{1,0},{2,1},{3,2},{4,7},{5,4},{6,5},{7,6},{8,11},{9,8},{10,9... | collective-permute-start | bytes 36872 | tf_op jit(solution)/shard_map/ppermute | solution.py:20
  43.9 4.3 %collective-permute-start.10 = (bf16[6,32,256]{2,1,0:T(8,128)(2,1)S(1)}, bf16[6,32,256]{2,1,0:T(8,128)(2,1)S(1)}, u32[]{:S(2)}, u32[]{:S(2)}) collective-permute-start(bf16[6,32,256]{2,1,0:T(8,128)(2,1)S(1)} %get-tuple-element.25), channel_id=1, source_target_pairs={{0,12},{4,0},{8,4},{12,8},{1,13},{5,1},{9,5},{13,9},{2,14},{6,2},{... | collective-permute-start | bytes 294920 | tf_op jit(solution)/shard_map/ppermute | solution.py:20
  48.3 0.6 collective-permute-start.6
  49.2 3.2 %collective-permute-start.11 = (bf16[6,38,256]{2,1,0:T(8,128)(2,1)S(1)}, bf16[6,38,256]{2,1,0:T(8,128)(2,1)S(1)}, u32[]{:S(2)}, u32[]{:S(2)}) collective-permute-start(bf16[6,38,256]{2,1,0:T(8,128)(2,1)S(1)} %get-tuple-element.23), channel_id=1, source_target_pairs={{0,12},{4,0},{8,4},{12,8},{1,13},{5,1},{9,5},{13,9},{2,14},{6,2},{... | collective-permute-start | bytes 350216 | tf_op jit(solution)/shard_map/ppermute | solution.py:20
  52.4 1.1 %collective-permute-start.9 = (bf16[6,38,256]{2,1,0:T(8,128)(2,1)S(1)}, bf16[6,38,256]{2,1,0:T(8,128)(2,1)S(1)}, u32[]{:S(2)}, u32[]{:S(2)}) collective-permute-start(bf16[6,38,256]{2,1,0:T(8,128)(2,1)S(1)} %get-tuple-element.24), channel_id=1, source_target_pairs={{0,8},{4,12},{8,0},{12,4},{1,9},{5,13},{9,1},{13,5},{2,10},{6,14},... | collective-permute-start | bytes 350216 | tf_op jit(solution)/shard_map/ppermute | solution.py:20
  53.6 3.4 %collective-permute-done.6 = bf16[262,256]{1,0:T(8,128)(2,1)S(1)} collective-permute-done((bf16[262,256]{1,0:T(8,128)(2,1)S(1)}, bf16[262,256]{1,0:T(8,128)(2,1)S(1)}, u32[]{:S(2)}, u32[]{:S(2)}) %collective-permute-start.6) | collective-permute-done | bytes 134176 | tf_op jit(solution)/shard_map/ppermute | solution.py:20
  57.0 7.3 %collective-permute-start.7 = (bf16[6,38,256]{2,1,0:T(8,128)(2,1)S(1)}, bf16[6,38,256]{2,1,0:T(8,128)(2,1)S(1)}, u32[]{:S(2)}, u32[]{:S(2)}) collective-permute-start(bf16[6,38,256]{2,1,0:T(8,128)(2,1)S(1)} %get-tuple-element.27), channel_id=1, source_target_pairs={{0,4},{4,8},{8,12},{12,0},{1,5},{5,9},{9,13},{13,1},{2,6},{6,10},{... | collective-permute-start | bytes 350216 | tf_op jit(solution)/shard_map/ppermute | solution.py:20
  64.4 4.1 %collective-permute-done.9.before_out_ref = bf16[6,38,256]{2,1,0:T(8,128)(2,1)S(1)} collective-permute-done((bf16[6,38,256]{2,1,0:T(8,128)(2,1)S(1)}, bf16[6,38,256]{2,1,0:T(8,128)(2,1)S(1)}, u32[]{:S(2)}, u32[]{:S(2)}) %collective-permute-start.9) | collective-permute-done | bytes 116768 | tf_op jit(solution)/shard_map/ppermute | solution.py:20
  68.4 2.2 %early_steps.1 = (bf16[2,64,256]{2,1,0:T(8,128)(2,1)S(1)}, f32[17,80,256]{2,1,0:T(8,128)S(1)}) custom-call(f32[2,3]{1,0:T(2,128)S(1)} %slice_multiply_fusion.links_ref, f32[4]{0:T(128)S(1)} %copy-done, s32[1]{0:T(128)} %bitcast.depth_ref, f32[4,32,256]{2,1,0:T(8,128)S(1)} %flows.2.middle_ref, f32[4,38,256]{2,1,0:T(8,128)S(1)} %pad_maximum_fusion.edge_ref, ...), custom_call_target="tpu_custom_call" | custom-call | flops 8388608 | bytes 2097152 | tf_op jit(solution)/shard_map/early_steps/pallas_call | solution.py:398
  70.7 0.8 %collective-permute-start.13 = (bf16[2,64,256]{2,1,0:T(8,128)(2,1)S(1)}, bf16[2,64,256]{2,1,0:T(8,128)(2,1)S(1)}, u32[]{:S(2)}, u32[]{:S(2)}) collective-permute-start(bf16[2,64,256]{2,1,0:T(8,128)(2,1)S(1)} %get-tuple-element.4), channel_id=1, source_target_pairs={{0,4},{4,8},{8,12},{12,0},{1,5},{5,9},{9,13},{13,1},{2,6},{6,10},{... | collective-permute-start | bytes 196616 | tf_op jit(solution)/shard_map/ppermute | solution.py:20
  71.5 3.1 %collective-permute-start.12 = (bf16[2,64,256]{2,1,0:T(8,128)(2,1)S(1)}, bf16[2,64,256]{2,1,0:T(8,128)(2,1)S(1)}, u32[]{:S(2)}, u32[]{:S(2)}) collective-permute-start(bf16[2,64,256]{2,1,0:T(8,128)(2,1)S(1)} %get-tuple-element.4), channel_id=1, source_target_pairs={{0,12},{4,0},{8,4},{12,8},{1,13},{5,1},{9,5},{13,9},{2,14},{6,2},{... | collective-permute-start | bytes 196616 | tf_op jit(solution)/shard_map/ppermute | solution.py:20
  74.5 0.7 maximum_bitcast_fusion
  75.2 1.7 %collective-permute-done.13.down_ref = bf16[2,64,256]{2,1,0:T(8,128)(2,1)S(1)} collective-permute-done((bf16[2,64,256]{2,1,0:T(8,128)(2,1)S(1)}, bf16[2,64,256]{2,1,0:T(8,128)(2,1)S(1)}, u32[]{:S(2)}, u32[]{:S(2)}) %collective-permute-start.13) | collective-permute-done | bytes 65568 | tf_op jit(solution)/shard_map/ppermute | solution.py:20
  76.9 1.1 %last_step.1 = f32[2,64,256]{2,1,0:T(8,128)} custom-call(bf16[2,64,256]{2,1,0:T(8,128)(2,1)S(1)} %collective-permute-done.12.up_ref, bf16[2,64,256]{2,1,0:T(8,128)(2,1)S(1)} %collective-permute-done.13.down_ref, f32[17,80,256]{2,1,0:T(8,128)S(1)} %get-tuple-element.5.state_ref), custom_call_target="tpu_custom_call" | custom-call | flops 4194304 | bytes 2097152 | tf_op jit(solution)/shard_map/last_step/pallas_call | solution.py:412
  (65 shorter events, 2.0 us)
Async XLA Ops:
  0.6 10.2 %copy-start.1 = (s32[1,64,256]{2,1,0:T(8,128)S(1)}, s32[1,64,256]{2,1,0:T(8,128)}, u32[]{:S(2)}) copy-start(s32[1,64,256]{2,1,0:T(8,128)} %param.5) | copy-start | bytes 196612
  0.6 9.3 %copy-start.2 = (s32[4,4]{1,0:T(4,128)S(1)}, s32[4,4]{1,0:T(4,128)}, u32[]{:S(2)}) copy-start(s32[4,4]{1,0:T(4,128)} %param.7) | copy-start | bytes 196
  2.9 9.1 %collective-permute-start.1 = (bf16[7,16,256]{2,1,0:T(8,128)(2,1)S(1)}, bf16[7,16,256]{2,1,0:T(8,128)(2,1)S(1)}, u32[]{:S(2)}, u32[]{:S(2)}) collective-permute-start(bf16[7,16,256]{2,1,0:T(8,128)(2,1)S(1)} %pad_maximum_fusion.10), channel_id=1, source_target_pairs={{0,1},{1,2},{2,3},{3,0},{4,5},{5,6},{6,7},{7,4},{8,9},{9,10},{10,1... | collective-permute-start | bytes 172040 | tf_op jit(solution)/shard_map/ppermute | solution.py:20
  3.5 8.6 %collective-permute-start.2 = (bf16[7,16,256]{2,1,0:T(8,128)(2,1)S(1)}, bf16[7,16,256]{2,1,0:T(8,128)(2,1)S(1)}, u32[]{:S(2)}, u32[]{:S(2)}) collective-permute-start(bf16[7,16,256]{2,1,0:T(8,128)(2,1)S(1)} %pad_maximum_fusion.11), channel_id=1, source_target_pairs={{0,3},{1,0},{2,1},{3,2},{4,7},{5,4},{6,5},{7,6},{8,11},{9,8},{10,9... | collective-permute-start | bytes 172040 | tf_op jit(solution)/shard_map/ppermute | solution.py:20
  5.5 13.2 %collective-permute-start = (bf16[44,16,256]{2,1,0:T(8,128)(2,1)S(1)}, bf16[44,16,256]{2,1,0:T(8,128)(2,1)S(1)}, u32[]{:S(2)}, u32[]{:S(2)}) collective-permute-start(bf16[44,16,256]{2,1,0:T(8,128)(2,1)S(1)} %slice.151), channel_id=1, source_target_pairs={{0,12},{4,0},{8,4},{12,8},{1,13},{5,1},{9,5},{13,9},{2,14},{6,2},{... | collective-permute-start | bytes 1081352 | tf_op jit(solution)/shard_map/ppermute | solution.py:20
  12.2 18.6 %collective-permute-start.3 = (bf16[37,16,256]{2,1,0:T(8,128)(2,1)S(1)}, bf16[37,16,256]{2,1,0:T(8,128)(2,1)S(1)}, u32[]{:S(2)}, u32[]{:S(2)}) collective-permute-start(bf16[37,16,256]{2,1,0:T(8,128)(2,1)S(1)} %constant_dynamic-update-slice_fusion), channel_id=1, source_target_pairs={{0,12},{4,0},{8,4},{12,8},{1,13},{5,1},{9,5},{13,9},{2,14},{6,2},{... | collective-permute-start | bytes 909320 | tf_op jit(solution)/shard_map/ppermute | solution.py:20
  42.1 26.4 %copy-start = (f32[4]{0:T(128)S(1)}, f32[4]{0:T(128)}, u32[]{:S(2)}) copy-start(f32[4]{0:T(128)} %stiffness_ref.1) | copy-start | bytes 52
  42.1 6.8 %collective-permute-start.4 = (f32[4,3,256]{2,1,0:T(4,128)S(1)}, f32[4,3,256]{2,1,0:T(4,128)S(1)}, u32[]{:S(2)}, u32[]{:S(2)}) collective-permute-start(f32[4,3,256]{2,1,0:T(4,128)S(1)} %get-tuple-element.21), channel_id=1, source_target_pairs={{0,1},{1,2},{2,3},{3,0},{4,5},{5,6},{6,7},{7,4},{8,9},{9,10},{10,1... | collective-permute-start | bytes 36872 | tf_op jit(solution)/shard_map/ppermute | solution.py:20
  42.2 6.7 %collective-permute-start.5 = (f32[4,3,256]{2,1,0:T(4,128)S(1)}, f32[4,3,256]{2,1,0:T(4,128)S(1)}, u32[]{:S(2)}, u32[]{:S(2)}) collective-permute-start(f32[4,3,256]{2,1,0:T(4,128)S(1)} %get-tuple-element.22), channel_id=1, source_target_pairs={{0,3},{1,0},{2,1},{3,2},{4,7},{5,4},{6,5},{7,6},{8,11},{9,8},{10,9... | collective-permute-start | bytes 36872 | tf_op jit(solution)/shard_map/ppermute | solution.py:20
  43.9 20.4 %collective-permute-start.10 = (bf16[6,32,256]{2,1,0:T(8,128)(2,1)S(1)}, bf16[6,32,256]{2,1,0:T(8,128)(2,1)S(1)}, u32[]{:S(2)}, u32[]{:S(2)}) collective-permute-start(bf16[6,32,256]{2,1,0:T(8,128)(2,1)S(1)} %get-tuple-element.25), channel_id=1, source_target_pairs={{0,12},{4,0},{8,4},{12,8},{1,13},{5,1},{9,5},{13,9},{2,14},{6,2},{... | collective-permute-start | bytes 294920 | tf_op jit(solution)/shard_map/ppermute | solution.py:20
  48.3 16.1 %collective-permute-start.8 = (bf16[6,32,256]{2,1,0:T(8,128)(2,1)S(1)}, bf16[6,32,256]{2,1,0:T(8,128)(2,1)S(1)}, u32[]{:S(2)}, u32[]{:S(2)}) collective-permute-start(bf16[6,32,256]{2,1,0:T(8,128)(2,1)S(1)} %get-tuple-element.26), channel_id=1, source_target_pairs={{0,8},{4,12},{8,0},{12,4},{1,9},{5,13},{9,1},{13,5},{2,10},{6,14},... | collective-permute-start | bytes 294920 | tf_op jit(solution)/shard_map/ppermute | solution.py:20
  48.3 8.7 %collective-permute-start.6 = (bf16[262,256]{1,0:T(8,128)(2,1)S(1)}, bf16[262,256]{1,0:T(8,128)(2,1)S(1)}, u32[]{:S(2)}, u32[]{:S(2)}) collective-permute-start(bf16[262,256]{1,0:T(8,128)(2,1)S(1)} %pad_maximum_fusion.1), channel_id=1, source_target_pairs={{0,4},{4,8},{8,12},{12,0},{1,5},{5,9},{9,13},{13,1},{2,6},{6,10},{... | collective-permute-start | bytes 402440 | tf_op jit(solution)/shard_map/ppermute | solution.py:20
  49.2 15.1 %collective-permute-start.11 = (bf16[6,38,256]{2,1,0:T(8,128)(2,1)S(1)}, bf16[6,38,256]{2,1,0:T(8,128)(2,1)S(1)}, u32[]{:S(2)}, u32[]{:S(2)}) collective-permute-start(bf16[6,38,256]{2,1,0:T(8,128)(2,1)S(1)} %get-tuple-element.23), channel_id=1, source_target_pairs={{0,12},{4,0},{8,4},{12,8},{1,13},{5,1},{9,5},{13,9},{2,14},{6,2},{... | collective-permute-start | bytes 350216 | tf_op jit(solution)/shard_map/ppermute | solution.py:20
  52.4 16.0 %collective-permute-start.9 = (bf16[6,38,256]{2,1,0:T(8,128)(2,1)S(1)}, bf16[6,38,256]{2,1,0:T(8,128)(2,1)S(1)}, u32[]{:S(2)}, u32[]{:S(2)}) collective-permute-start(bf16[6,38,256]{2,1,0:T(8,128)(2,1)S(1)} %get-tuple-element.24), channel_id=1, source_target_pairs={{0,8},{4,12},{8,0},{12,4},{1,9},{5,13},{9,1},{13,5},{2,10},{6,14},... | collective-permute-start | bytes 350216 | tf_op jit(solution)/shard_map/ppermute | solution.py:20
  57.0 11.5 %collective-permute-start.7 = (bf16[6,38,256]{2,1,0:T(8,128)(2,1)S(1)}, bf16[6,38,256]{2,1,0:T(8,128)(2,1)S(1)}, u32[]{:S(2)}, u32[]{:S(2)}) collective-permute-start(bf16[6,38,256]{2,1,0:T(8,128)(2,1)S(1)} %get-tuple-element.27), channel_id=1, source_target_pairs={{0,4},{4,8},{8,12},{12,0},{1,5},{5,9},{9,13},{13,1},{2,6},{6,10},{... | collective-permute-start | bytes 350216 | tf_op jit(solution)/shard_map/ppermute | solution.py:20
  70.7 6.3 %collective-permute-start.13 = (bf16[2,64,256]{2,1,0:T(8,128)(2,1)S(1)}, bf16[2,64,256]{2,1,0:T(8,128)(2,1)S(1)}, u32[]{:S(2)}, u32[]{:S(2)}) collective-permute-start(bf16[2,64,256]{2,1,0:T(8,128)(2,1)S(1)} %get-tuple-element.4), channel_id=1, source_target_pairs={{0,4},{4,8},{8,12},{12,0},{1,5},{5,9},{9,13},{13,1},{2,6},{6,10},{... | collective-permute-start | bytes 196616 | tf_op jit(solution)/shard_map/ppermute | solution.py:20
  71.5 5.5 %collective-permute-start.12 = (bf16[2,64,256]{2,1,0:T(8,128)(2,1)S(1)}, bf16[2,64,256]{2,1,0:T(8,128)(2,1)S(1)}, u32[]{:S(2)}, u32[]{:S(2)}) collective-permute-start(bf16[2,64,256]{2,1,0:T(8,128)(2,1)S(1)} %get-tuple-element.4), channel_id=1, source_target_pairs={{0,12},{4,0},{8,4},{12,8},{1,13},{5,1},{9,5},{13,9},{2,14},{6,2},{... | collective-permute-start | bytes 196616 | tf_op jit(solution)/shard_map/ppermute | solution.py:20
where the time goes:
time: 78.2 us; the launch traced here: 78 us
  starting transfers between devices  29.8 us (38%)
  Pallas kernels  25.8 us (33%)
  waiting for transfers between devices  15.2 us (19%)
  other arithmetic  2.89 us (4%)
  local copies, waits for them, and re-layouts  2.68 us (3%)
  between operations  1.58 us (2%)
    ppermute x14, starting transfers between devices, ringed(): lax.ppermute(value, axis, [(i, (i + steps) % count) for i in range(count)])  29.8 us
    pallas_call x2, Pallas kernels, flows(): pl.pallas_call(functools.partial(flow_kernel, *tables, len(early)), out_s...  22.5 us
    ppermute x14, waiting for transfers between devices, ringed(): lax.ppermute(value, axis, [(i, (i + steps) % count) for i in range(count)])  15.2 us
    pallas_call x1, Pallas kernels, relaxation(): pl.pallas_call(early_kernel, out_shape=(jax.ShapeDtypeStruct(change_shape...  2.22 us
  transfers between devices with their start and end apart: 14, of which 4 were waited for; matrix products, arithmetic and copies ran while one was open for 4% of the time, Pallas kernels for 14%

commit v1 on v0

--- a/solution.py
+++ b/solution.py
@@ -223,6 +223,12 @@
     return vector / jnp.sqrt(1.0 + squares / (saturation * saturation))
 
 
+def swapped(value, axis, parity):
+    firsts = range(parity, lax.axis_size(axis) - 1, 2)
+    pairs = [(i + k, i + 1 - k) for i in firsts for k in range(2)]
+    return lax.ppermute(value, axis, pairs)
+
+
 def pair_part(apart, here, forward, ahead):
     return step_size * here * (spring(apart - forward) - spring(-apart - ahead))
 
@@ -255,8 +261,8 @@
 
 
 def spring_pair(row, col):
-    length = jnp.sqrt(1.0 + (row * row + col * col) / (saturation * saturation))
-    return row / length, col / length
+    inverse = lax.rsqrt(1.0 + (row * row + col * col) * (1.0 / (saturation * saturation)))
+    return row * inverse, col * inverse
 
 
 def pair_pull(apart, here, forward, ahead):
@@ -291,7 +297,7 @@
 
 
 def early_kernel(
-    links_ref, stiffness_ref, depth_ref, middle_ref, edge_ref, below_mid_ref, below_out_ref, before_mid_ref,
+    deep, links_ref, stiffness_ref, depth_ref, middle_ref, edge_ref, below_mid_ref, below_out_ref, before_mid_ref,
     before_out_ref, above_mid_ref, above_out_ref, own_ref, upper_ref, lower_ref, change_ref, state_ref, frame_ref
 ):
     rows, cols = state_ref.shape[1:]
@@ -342,7 +348,7 @@
     far = [jnp.where(depth_ref[0] > 1, h + r, 0.0) for h, r in zip(high, rest)]
     part_before = fields(before_mid_ref, before_out_ref, 4)
     part_above = fields(above_mid_ref, above_out_ref, 0)
-    if above_mid_ref.shape[0] > 2:
+    if not deep:
         high, rest = fields(above_mid_ref, above_out_ref, 2), fields(above_mid_ref, above_out_ref, 4)
         far = [f + jnp.where(depth_ref[0] > 2, h + r, 0.0) for f, h, r in zip(far, high, rest)]
 
@@ -370,7 +376,7 @@
         state_ref[i] = value
 
 
-def late_kernel(up_ref, down_ref, state_ref, out_ref):
+def late_kernel(depth_ref, even_ref, odd_ref, state_ref, out_ref):
     rows, cols = state_ref.shape[1:]
     height = rows - 2 * FRAME
     body = slice(FRAME, FRAME + height)
@@ -384,8 +390,10 @@
         return [state_ref[at + i, body, :] for i in range(2)]
 
     mid = two(0)
-    up = [a + up_ref[i].astype(jnp.float32) - m for i, (a, m) in enumerate(zip(two(2), mid))]
-    down = [m - a - down_ref[i].astype(jnp.float32) for i, (a, m) in enumerate(zip(two(4), mid))]
+    first_of_pair = depth_ref[0] % 2 == 0
+    swaps = [(even_ref[i].astype(jnp.float32), odd_ref[i].astype(jnp.float32)) for i in range(2)]
+    up = [a + jnp.where(first_of_pair, e, o) - m for a, m, (e, o) in zip(two(2), mid, swaps)]
+    down = [m - a - jnp.where(first_of_pair, o, e) for a, m, (e, o) in zip(two(4), mid, swaps)]
     pull = pair_pull(up, state_ref[14, body, :], two(6), two(8))
     push = pair_pull(down, state_ref[15, body, :], two(10), two(12))
     for i in range(2):
@@ -396,7 +404,7 @@
     height, breadth = change_shape[1:]
     vmem, smem = pl.BlockSpec(memory_space=pltpu.VMEM), pl.BlockSpec(memory_space=pltpu.SMEM)
     change, state = pl.pallas_call(
-        early_kernel,
+        functools.partial(early_kernel, lax.axis_size("gz") > 4),
         out_shape=(
             jax.ShapeDtypeStruct(change_shape, jnp.bfloat16),
             jax.ShapeDtypeStruct((17, height + 2 * FRAME, breadth), jnp.float32),
@@ -408,16 +416,17 @@
         cost_estimate=pl.CostEstimate(flops=2**23, bytes_accessed=2**21, transcendentals=2**16),
         name="early_steps",
     )(links, stiffness, depth, *arrays)
-    up, down = ringed(change, "gz", -1), ringed(change, "gz", 1)
+    even = swapped(change, "gz", 0)
+    odd = swapped(change, "gz", 1)
     return pl.pallas_call(
         late_kernel,
         out_shape=jax.ShapeDtypeStruct(change_shape, jnp.float32),
-        in_specs=[vmem] * 3,
+        in_specs=[smem] + [vmem] * 3,
         out_specs=vmem,
         compiler_params=pltpu.CompilerParams(vmem_limit_bytes=16 * 2**20),
         cost_estimate=pl.CostEstimate(flops=2**22, bytes_accessed=2**21, transcendentals=2**15),
         name="last_step",
-    )(up, down, state)
+    )(depth, even, odd, state)
 
 
 def whole_device(features, class_map, stiffness, valid):

time: 78.2 us -> 79.2 us (1.013)
  starting transfers between devices: 29.8 us -> 31.1 us
    ppermute x0 -> x2, starting transfers between devices: none -> 5.17 us  [swapped(): return lax.ppermute(value, axis, pairs)]
    ppermute x14 -> x12, starting transfers between devices: 29.8 us -> 25.9 us  [ringed(): lax.ppermute(value, axis, [(i, (i + steps) % count) for i in range(count)])]
    ppermute x14 -> x12, waiting for transfers between devices: 15.2 us -> 13.5 us  [ringed(): lax.ppermute(value, axis, [(i, (i + steps) % count) for i in range(count)])]
    ppermute x0 -> x2, waiting for transfers between devices: none -> 1.58 us  [swapped(): return lax.ppermute(value, axis, pairs)]
where the time goes in v1:
time: 79.2 us; the launch traced here: 79 us
  starting transfers between devices  31.1 us (39%)
  Pallas kernels  25.6 us (32%)
  waiting for transfers between devices  15.1 us (19%)
  other arithmetic  2.92 us (4%)
  local copies, waits for them, and re-layouts  2.62 us (3%)
  between operations  1.61 us (2%)
    ppermute x12, starting transfers between devices, ringed(): lax.ppermute(value, axis, [(i, (i + steps) % count) for i in range(count)])  25.9 us
    pallas_call x2, Pallas kernels, flows(): pl.pallas_call(functools.partial(flow_kernel, *tables, len(early)), out_s...  22.5 us
    ppermute x12, waiting for transfers between devices, ringed(): lax.ppermute(value, axis, [(i, (i + steps) % count) for i in range(count)])  13.5 us
    ppermute x2, starting transfers between devices, swapped(): return lax.ppermute(value, axis, pairs)  5.17 us
    pallas_call x1, Pallas kernels, relaxation(): pl.pallas_call(functools.partial(early_kernel, lax.axis_size('gz') > 4),...  2.07 us
  transfers between devices with their start and end apart: 14, of which 4 were waited for; matrix products, arithmetic and copies ran while one was open for 4% of the time, Pallas kernels for 14%

profile of v1, /device:TPU:0, one launch (start us, length us, event | category | flops | bytes accessed | tf_op | source)
XLA Modules:
  0.0 79.0 jit_solution(248916801253951092)
XLA Ops:
  0.6 0.9 %add_convert_fusion = bf16[1,64,256]{2,1,0:T(8,128)(2,1)S(1)} fusion(s32[1,64,256]{2,1,0:T(8,128)} %param.5), kind=kLoop, calls=%fused_computation.32 | loop fusion | flops 32768 | bytes 98304 | tf_op jit(solution)/shard_map/convert_element_type | solution.py:442
  1.6 1.3 %copy.9 = bf16[1,16,64,256]{3,1,2,0:T(8,128)(2,1)S(1)} copy(bf16[1,16,64,256]{3,2,1,0:T(8,128)(2,1)} %param.4) | data formatting | bytes 1048576 | tf_op args[0]
  2.9 0.5 collective-permute-start.1
  3.5 2.0 %collective-permute-start.2 = (bf16[7,16,256]{2,1,0:T(8,128)(2,1)S(1)}, bf16[7,16,256]{2,1,0:T(8,128)(2,1)S(1)}, u32[]{:S(2)}, u32[]{:S(2)}) collective-permute-start(bf16[7,16,256]{2,1,0:T(8,128)(2,1)S(1)} %pad_maximum_fusion.11), channel_id=1, source_target_pairs={{0,3},{1,0},{2,1},{3,2},{4,7},{5,4},{6,5},{7,6},{8,11},{9,8},{10,9... | collective-permute-start | bytes 172040 | tf_op jit(solution)/shard_map/ppermute | solution.py:20
  5.5 4.4 %collective-permute-start = (bf16[44,16,256]{2,1,0:T(8,128)(2,1)S(1)}, bf16[44,16,256]{2,1,0:T(8,128)(2,1)S(1)}, u32[]{:S(2)}, u32[]{:S(2)}) collective-permute-start(bf16[44,16,256]{2,1,0:T(8,128)(2,1)S(1)} %slice.151), channel_id=1, source_target_pairs={{0,12},{4,0},{8,4},{12,8},{1,13},{5,1},{9,5},{13,9},{2,14},{6,2},{... | collective-permute-start | bytes 1081352 | tf_op jit(solution)/shard_map/ppermute | solution.py:20
  10.0 0.6 slice.134
  12.7 6.1 %collective-permute-done.refs_1_.refs_3_ = bf16[44,16,256]{2,1,0:T(8,128)(2,1)S(1)} collective-permute-done((bf16[44,16,256]{2,1,0:T(8,128)(2,1)S(1)}, bf16[44,16,256]{2,1,0:T(8,128)(2,1)S(1)}, u32[]{:S(2)}, u32[]{:S(2)}) %collective-permute-start) | collective-permute-done | bytes 360480 | tf_op jit(solution)/shard_map/ppermute | solution.py:20
  18.7 11.3 %flows.2.middle_ref = f32[4,32,256]{2,1,0:T(8,128)S(1)} custom-call(f32[1]{0:T(128)} %bitcast.1.live_ref, bf16[64,16,256]{2,1,0:T(8,128)(2,1)S(1)} %bitcast.36, bf16[44,16,256]{2,1,0:T(8,128)(2,1)S(1)} %collective-permute-done.refs_1_.refs_3_), custom_call_target="tpu_custom_call" | custom-call | flops 2147483648 | bytes 4194304 | tf_op jit(solution)/shard_map/flows/pallas_call | solution.py:200
  30.0 0.7 multiply_reduce_fusion.3
  30.8 11.3 %flows.3 = f32[4,32,256]{2,1,0:T(8,128)S(1)} custom-call(f32[1]{0:T(128)} %bitcast.1.live_ref, bf16[64,16,256]{2,1,0:T(8,128)(2,1)S(1)} %bitcast.37, bf16[7,16,256]{2,1,0:T(8,128)(2,1)S(1)} %broadcast_select_fusion.1.refs_1_, bf16[7,16,256]{2,1,0:T(8,128)(2,1)S(1)} %broadcast_select_fusion.refs_2_, ...), custom_call_target="tpu_custom_call" | custom-call | flops 2147483648 | bytes 4194304 | tf_op jit(solution)/shard_map/flows/pallas_call | solution.py:200
  42.2 1.7 %collective-permute-start.5 = (f32[4,3,256]{2,1,0:T(4,128)S(1)}, f32[4,3,256]{2,1,0:T(4,128)S(1)}, u32[]{:S(2)}, u32[]{:S(2)}) collective-permute-start(f32[4,3,256]{2,1,0:T(4,128)S(1)} %get-tuple-element.22), channel_id=1, source_target_pairs={{0,3},{1,0},{2,1},{3,2},{4,7},{5,4},{6,5},{7,6},{8,11},{9,8},{10,9... | collective-permute-start | bytes 36872 | tf_op jit(solution)/shard_map/ppermute | solution.py:20
  44.0 4.3 %collective-permute-start.10 = (bf16[6,32,256]{2,1,0:T(8,128)(2,1)S(1)}, bf16[6,32,256]{2,1,0:T(8,128)(2,1)S(1)}, u32[]{:S(2)}, u32[]{:S(2)}) collective-permute-start(bf16[6,32,256]{2,1,0:T(8,128)(2,1)S(1)} %get-tuple-element.25), channel_id=1, source_target_pairs={{0,12},{4,0},{8,4},{12,8},{1,13},{5,1},{9,5},{13,9},{2,14},{6,2},{... | collective-permute-start | bytes 294920 | tf_op jit(solution)/shard_map/ppermute | solution.py:20
  48.3 0.6 collective-permute-start.6
  49.2 3.2 %collective-permute-start.11 = (bf16[6,38,256]{2,1,0:T(8,128)(2,1)S(1)}, bf16[6,38,256]{2,1,0:T(8,128)(2,1)S(1)}, u32[]{:S(2)}, u32[]{:S(2)}) collective-permute-start(bf16[6,38,256]{2,1,0:T(8,128)(2,1)S(1)} %get-tuple-element.23), channel_id=1, source_target_pairs={{0,12},{4,0},{8,4},{12,8},{1,13},{5,1},{9,5},{13,9},{2,14},{6,2},{... | collective-permute-start | bytes 350216 | tf_op jit(solution)/shard_map/ppermute | solution.py:20
  52.5 1.1 %collective-permute-start.9 = (bf16[6,38,256]{2,1,0:T(8,128)(2,1)S(1)}, bf16[6,38,256]{2,1,0:T(8,128)(2,1)S(1)}, u32[]{:S(2)}, u32[]{:S(2)}) collective-permute-start(bf16[6,38,256]{2,1,0:T(8,128)(2,1)S(1)} %get-tuple-element.24), channel_id=1, source_target_pairs={{0,8},{4,12},{8,0},{12,4},{1,9},{5,13},{9,1},{13,5},{2,10},{6,14},... | collective-permute-start | bytes 350216 | tf_op jit(solution)/shard_map/ppermute | solution.py:20
  53.6 3.4 %collective-permute-done.6 = bf16[262,256]{1,0:T(8,128)(2,1)S(1)} collective-permute-done((bf16[262,256]{1,0:T(8,128)(2,1)S(1)}, bf16[262,256]{1,0:T(8,128)(2,1)S(1)}, u32[]{:S(2)}, u32[]{:S(2)}) %collective-permute-start.6) | collective-permute-done | bytes 134176 | tf_op jit(solution)/shard_map/ppermute | solution.py:20
  57.0 7.3 %collective-permute-start.7 = (bf16[6,38,256]{2,1,0:T(8,128)(2,1)S(1)}, bf16[6,38,256]{2,1,0:T(8,128)(2,1)S(1)}, u32[]{:S(2)}, u32[]{:S(2)}) collective-permute-start(bf16[6,38,256]{2,1,0:T(8,128)(2,1)S(1)} %get-tuple-element.27), channel_id=1, source_target_pairs={{0,4},{4,8},{8,12},{12,0},{1,5},{5,9},{9,13},{13,1},{2,6},{6,10},{... | collective-permute-start | bytes 350216 | tf_op jit(solution)/shard_map/ppermute | solution.py:20
  64.4 4.1 %collective-permute-done.9.before_out_ref = bf16[6,38,256]{2,1,0:T(8,128)(2,1)S(1)} collective-permute-done((bf16[6,38,256]{2,1,0:T(8,128)(2,1)S(1)}, bf16[6,38,256]{2,1,0:T(8,128)(2,1)S(1)}, u32[]{:S(2)}, u32[]{:S(2)}) %collective-permute-start.9) | collective-permute-done | bytes 116768 | tf_op jit(solution)/shard_map/ppermute | solution.py:20
  68.5 2.1 %early_steps.1 = (bf16[2,64,256]{2,1,0:T(8,128)(2,1)S(1)}, f32[17,80,256]{2,1,0:T(8,128)S(1)}) custom-call(f32[2,3]{1,0:T(2,128)S(1)} %slice_multiply_fusion.links_ref, f32[4]{0:T(128)S(1)} %copy-done, s32[1]{0:T(128)} %bitcast.depth_ref, f32[4,32,256]{2,1,0:T(8,128)S(1)} %flows.2.middle_ref, f32[4,38,256]{2,1,0:T(8,128)S(1)} %pad_maximum_fusion.edge_ref, ...), custom_call_target="tpu_custom_call" | custom-call | flops 8388608 | bytes 2097152 | tf_op jit(solution)/shard_map/early_steps/pallas_call | solution.py:406
  70.5 0.7 collective-permute-start.13
  71.2 4.5 %collective-permute-start.12 = (bf16[2,64,256]{2,1,0:T(8,128)(2,1)S(1)}, bf16[2,64,256]{2,1,0:T(8,128)(2,1)S(1)}, u32[]{:S(2)}, u32[]{:S(2)}) collective-permute-start(bf16[2,64,256]{2,1,0:T(8,128)(2,1)S(1)} %get-tuple-element.4), channel_id=1, source_target_pairs={{0,4},{4,0},{8,12},{12,8},{1,5},{5,1},{9,13},{13,9},{2,6},{6,2},{1... | collective-permute-start | bytes 196616 | tf_op jit(solution)/shard_map/ppermute | solution.py:229
  75.7 0.7 maximum_bitcast_fusion
  76.4 1.6 %collective-permute-done.12.even_ref = bf16[2,64,256]{2,1,0:T(8,128)(2,1)S(1)} collective-permute-done((bf16[2,64,256]{2,1,0:T(8,128)(2,1)S(1)}, bf16[2,64,256]{2,1,0:T(8,128)(2,1)S(1)}, u32[]{:S(2)}, u32[]{:S(2)}) %collective-permute-start.12) | collective-permute-done | bytes 65568 | tf_op jit(solution)/shard_map/ppermute | solution.py:229
  78.0 1.0 %last_step.1 = f32[2,64,256]{2,1,0:T(8,128)} custom-call(s32[1]{0:T(128)} %bitcast.depth_ref, bf16[2,64,256]{2,1,0:T(8,128)(2,1)S(1)} %collective-permute-done.12.even_ref, bf16[2,64,256]{2,1,0:T(8,128)(2,1)S(1)} %collective-permute-done.13.odd_ref, f32[17,80,256]{2,1,0:T(8,128)S(1)} %get-tuple-element.5.state_ref), custom_call_target="tpu_custom_call" | custom-call | flops 4194304 | bytes 2097152 | tf_op jit(solution)/shard_map/last_step/pallas_call | solution.py:421
  (65 shorter events, 2.0 us)
Async XLA Ops:
  0.6 10.2 %copy-start.1 = (s32[1,64,256]{2,1,0:T(8,128)S(1)}, s32[1,64,256]{2,1,0:T(8,128)}, u32[]{:S(2)}) copy-start(s32[1,64,256]{2,1,0:T(8,128)} %param.5) | copy-start | bytes 196612
  0.6 9.3 %copy-start.2 = (s32[4,4]{1,0:T(4,128)S(1)}, s32[4,4]{1,0:T(4,128)}, u32[]{:S(2)}) copy-start(s32[4,4]{1,0:T(4,128)} %param.7) | copy-start | bytes 196
  2.9 9.1 %collective-permute-start.1 = (bf16[7,16,256]{2,1,0:T(8,128)(2,1)S(1)}, bf16[7,16,256]{2,1,0:T(8,128)(2,1)S(1)}, u32[]{:S(2)}, u32[]{:S(2)}) collective-permute-start(bf16[7,16,256]{2,1,0:T(8,128)(2,1)S(1)} %pad_maximum_fusion.10), channel_id=1, source_target_pairs={{0,1},{1,2},{2,3},{3,0},{4,5},{5,6},{6,7},{7,4},{8,9},{9,10},{10,1... | collective-permute-start | bytes 172040 | tf_op jit(solution)/shard_map/ppermute | solution.py:20
  3.5 8.6 %collective-permute-start.2 = (bf16[7,16,256]{2,1,0:T(8,128)(2,1)S(1)}, bf16[7,16,256]{2,1,0:T(8,128)(2,1)S(1)}, u32[]{:S(2)}, u32[]{:S(2)}) collective-permute-start(bf16[7,16,256]{2,1,0:T(8,128)(2,1)S(1)} %pad_maximum_fusion.11), channel_id=1, source_target_pairs={{0,3},{1,0},{2,1},{3,2},{4,7},{5,4},{6,5},{7,6},{8,11},{9,8},{10,9... | collective-permute-start | bytes 172040 | tf_op jit(solution)/shard_map/ppermute | solution.py:20
  5.5 13.2 %collective-permute-start = (bf16[44,16,256]{2,1,0:T(8,128)(2,1)S(1)}, bf16[44,16,256]{2,1,0:T(8,128)(2,1)S(1)}, u32[]{:S(2)}, u32[]{:S(2)}) collective-permute-start(bf16[44,16,256]{2,1,0:T(8,128)(2,1)S(1)} %slice.151), channel_id=1, source_target_pairs={{0,12},{4,0},{8,4},{12,8},{1,13},{5,1},{9,5},{13,9},{2,14},{6,2},{... | collective-permute-start | bytes 1081352 | tf_op jit(solution)/shard_map/ppermute | solution.py:20
  12.2 18.7 %collective-permute-start.3 = (bf16[37,16,256]{2,1,0:T(8,128)(2,1)S(1)}, bf16[37,16,256]{2,1,0:T(8,128)(2,1)S(1)}, u32[]{:S(2)}, u32[]{:S(2)}) collective-permute-start(bf16[37,16,256]{2,1,0:T(8,128)(2,1)S(1)} %constant_dynamic-update-slice_fusion), channel_id=1, source_target_pairs={{0,12},{4,0},{8,4},{12,8},{1,13},{5,1},{9,5},{13,9},{2,14},{6,2},{... | collective-permute-start | bytes 909320 | tf_op jit(solution)/shard_map/ppermute | solution.py:20
  42.1 26.4 %copy-start = (f32[4]{0:T(128)S(1)}, f32[4]{0:T(128)}, u32[]{:S(2)}) copy-start(f32[4]{0:T(128)} %stiffness_ref.1) | copy-start | bytes 52
  42.1 6.8 %collective-permute-start.4 = (f32[4,3,256]{2,1,0:T(4,128)S(1)}, f32[4,3,256]{2,1,0:T(4,128)S(1)}, u32[]{:S(2)}, u32[]{:S(2)}) collective-permute-start(f32[4,3,256]{2,1,0:T(4,128)S(1)} %get-tuple-element.21), channel_id=1, source_target_pairs={{0,1},{1,2},{2,3},{3,0},{4,5},{5,6},{6,7},{7,4},{8,9},{9,10},{10,1... | collective-permute-start | bytes 36872 | tf_op jit(solution)/shard_map/ppermute | solution.py:20
  42.2 6.7 %collective-permute-start.5 = (f32[4,3,256]{2,1,0:T(4,128)S(1)}, f32[4,3,256]{2,1,0:T(4,128)S(1)}, u32[]{:S(2)}, u32[]{:S(2)}) collective-permute-start(f32[4,3,256]{2,1,0:T(4,128)S(1)} %get-tuple-element.22), channel_id=1, source_target_pairs={{0,3},{1,0},{2,1},{3,2},{4,7},{5,4},{6,5},{7,6},{8,11},{9,8},{10,9... | collective-permute-start | bytes 36872 | tf_op jit(solution)/shard_map/ppermute | solution.py:20
  44.0 20.4 %collective-permute-start.10 = (bf16[6,32,256]{2,1,0:T(8,128)(2,1)S(1)}, bf16[6,32,256]{2,1,0:T(8,128)(2,1)S(1)}, u32[]{:S(2)}, u32[]{:S(2)}) collective-permute-start(bf16[6,32,256]{2,1,0:T(8,128)(2,1)S(1)} %get-tuple-element.25), channel_id=1, source_target_pairs={{0,12},{4,0},{8,4},{12,8},{1,13},{5,1},{9,5},{13,9},{2,14},{6,2},{... | collective-permute-start | bytes 294920 | tf_op jit(solution)/shard_map/ppermute | solution.py:20
  48.3 16.1 %collective-permute-start.8 = (bf16[6,32,256]{2,1,0:T(8,128)(2,1)S(1)}, bf16[6,32,256]{2,1,0:T(8,128)(2,1)S(1)}, u32[]{:S(2)}, u32[]{:S(2)}) collective-permute-start(bf16[6,32,256]{2,1,0:T(8,128)(2,1)S(1)} %get-tuple-element.26), channel_id=1, source_target_pairs={{0,8},{4,12},{8,0},{12,4},{1,9},{5,13},{9,1},{13,5},{2,10},{6,14},... | collective-permute-start | bytes 294920 | tf_op jit(solution)/shard_map/ppermute | solution.py:20
  48.3 8.7 %collective-permute-start.6 = (bf16[262,256]{1,0:T(8,128)(2,1)S(1)}, bf16[262,256]{1,0:T(8,128)(2,1)S(1)}, u32[]{:S(2)}, u32[]{:S(2)}) collective-permute-start(bf16[262,256]{1,0:T(8,128)(2,1)S(1)} %pad_maximum_fusion.1), channel_id=1, source_target_pairs={{0,4},{4,8},{8,12},{12,0},{1,5},{5,9},{9,13},{13,1},{2,6},{6,10},{... | collective-permute-start | bytes 402440 | tf_op jit(solution)/shard_map/ppermute | solution.py:20
  49.2 15.1 %collective-permute-start.11 = (bf16[6,38,256]{2,1,0:T(8,128)(2,1)S(1)}, bf16[6,38,256]{2,1,0:T(8,128)(2,1)S(1)}, u32[]{:S(2)}, u32[]{:S(2)}) collective-permute-start(bf16[6,38,256]{2,1,0:T(8,128)(2,1)S(1)} %get-tuple-element.23), channel_id=1, source_target_pairs={{0,12},{4,0},{8,4},{12,8},{1,13},{5,1},{9,5},{13,9},{2,14},{6,2},{... | collective-permute-start | bytes 350216 | tf_op jit(solution)/shard_map/ppermute | solution.py:20
  52.5 16.0 %collective-permute-start.9 = (bf16[6,38,256]{2,1,0:T(8,128)(2,1)S(1)}, bf16[6,38,256]{2,1,0:T(8,128)(2,1)S(1)}, u32[]{:S(2)}, u32[]{:S(2)}) collective-permute-start(bf16[6,38,256]{2,1,0:T(8,128)(2,1)S(1)} %get-tuple-element.24), channel_id=1, source_target_pairs={{0,8},{4,12},{8,0},{12,4},{1,9},{5,13},{9,1},{13,5},{2,10},{6,14},... | collective-permute-start | bytes 350216 | tf_op jit(solution)/shard_map/ppermute | solution.py:20
  57.0 11.5 %collective-permute-start.7 = (bf16[6,38,256]{2,1,0:T(8,128)(2,1)S(1)}, bf16[6,38,256]{2,1,0:T(8,128)(2,1)S(1)}, u32[]{:S(2)}, u32[]{:S(2)}) collective-permute-start(bf16[6,38,256]{2,1,0:T(8,128)(2,1)S(1)} %get-tuple-element.27), channel_id=1, source_target_pairs={{0,4},{4,8},{8,12},{12,0},{1,5},{5,9},{9,13},{13,1},{2,6},{6,10},{... | collective-permute-start | bytes 350216 | tf_op jit(solution)/shard_map/ppermute | solution.py:20
  70.5 5.8 %collective-permute-start.13 = (bf16[2,64,256]{2,1,0:T(8,128)(2,1)S(1)}, bf16[2,64,256]{2,1,0:T(8,128)(2,1)S(1)}, u32[]{:S(2)}, u32[]{:S(2)}) collective-permute-start(bf16[2,64,256]{2,1,0:T(8,128)(2,1)S(1)} %get-tuple-element.4), channel_id=1, source_target_pairs={{4,8},{8,4},{5,9},{9,5},{6,10},{10,6},{7,11},{11,7},{20,24},{24,20... | collective-permute-start | bytes 196616 | tf_op jit(solution)/shard_map/ppermute | solution.py:229
  71.2 6.8 %collective-permute-start.12 = (bf16[2,64,256]{2,1,0:T(8,128)(2,1)S(1)}, bf16[2,64,256]{2,1,0:T(8,128)(2,1)S(1)}, u32[]{:S(2)}, u32[]{:S(2)}) collective-permute-start(bf16[2,64,256]{2,1,0:T(8,128)(2,1)S(1)} %get-tuple-element.4), channel_id=1, source_target_pairs={{0,4},{4,0},{8,12},{12,8},{1,5},{5,1},{9,13},{13,9},{2,6},{6,2},{1... | collective-permute-start | bytes 196616 | tf_op jit(solution)/shard_map/ppermute | solution.py:229
